TPU v7x, 32 devices: a whole 2x2x4 slice. The times are simulated.
32 devices in a mesh: base: 16 (over z, x, core), chan: 2 (over y).
Axes of the slice: x: 2, y: 2, z: 4, core: 2. Of those that a mesh axis runs over, the one named last changes fastest.
Arguments:
- image0: float32 [2048, 2048], P(('base', 'chan')), may hold values from -6 to 6
- interp: float32 [16, 2, 256, 8, 256], P('base', 'chan'), may hold values from -0.375 to 0.375
- vis_weight: float32 [16, 2, 256, 8], P('base', 'chan'), may hold values from 0.2 to 5
- counts: int32 [16, 2, 256], P('base', 'chan'), may hold values from 1 to 8
- tile_index: int32 [16, 2, 256], P('base', 'chan'), may hold values from 0 to 511
Outputs:
- image_out: float32 [2048, 2048], P(('base', 'chan'))
- estimates: float32 [3], replicated
Inputs may be any that keep to these rules, and one draw needn't show every extreme that they name: `tile_index`: slot s of a device belongs to the spectrum block of device s // 8 of base+chan, base index major; the entry numbers the tile within that block. `counts`: visibility v of a slot is live when v < count.
All inputs are finite; a program needn't handle non-finite values.
Results may differ from a plain program's by a relative error of at most 0.00023.
Values sent between devices are 32-bit elements; how exact they have to be, the bound alone decides.
A program may use at most 128 MiB of HBM per device.

v0:
```python
import math
import jax
import jax.numpy as jnp
from jax import lax
from jax.sharding import PartitionSpec as P

TILE_V = 8
TILE_U = 32
ITERS = 3
PRECISION_LEVEL = lax.Precision.HIGHEST


def split_length(length):
    outer_len = 2 ** ((length.bit_length() - 1) // 2)
    return (outer_len, length // outer_len)


def angle_table(count_a, count_b, modulus, sign):
    left = jnp.arange(count_a, dtype=jnp.int32)[:, None]
    right = jnp.arange(count_b, dtype=jnp.int32)[None, :]
    angle = sign * 2.0 * math.pi / modulus * (left * right % modulus).astype(jnp.float32)
    return (jnp.cos(angle), jnp.sin(angle))


def transform_rows(real_part, imag_part, sign):
    row_count, length = real_part.shape
    outer_len, inner_len = split_length(length)
    cos_q, sin_q = angle_table(inner_len, inner_len, inner_len, sign)
    cos_t, sin_t = angle_table(inner_len, outer_len, length, sign)
    cos_p, sin_p = angle_table(outer_len, outer_len, outer_len, sign)
    real_in = real_part.reshape(row_count, inner_len, outer_len)
    first_re = jnp.einsum("kq,rqp->rkp", cos_q, real_in, precision=PRECISION_LEVEL)
    first_im = jnp.einsum("kq,rqp->rkp", sin_q, real_in, precision=PRECISION_LEVEL)
    if imag_part is not None:
        imag_in = imag_part.reshape(row_count, inner_len, outer_len)
        first_re = first_re - jnp.einsum("kq,rqp->rkp", sin_q, imag_in, precision=PRECISION_LEVEL)
        first_im = first_im + jnp.einsum("kq,rqp->rkp", cos_q, imag_in, precision=PRECISION_LEVEL)
    turned_re = first_re * cos_t - first_im * sin_t
    turned_im = first_re * sin_t + first_im * cos_t
    last_re = jnp.einsum("jp,rkp->rjk", cos_p, turned_re, precision=PRECISION_LEVEL) - jnp.einsum(
        "jp,rkp->rjk", sin_p, turned_im, precision=PRECISION_LEVEL
    )
    last_im = jnp.einsum("jp,rkp->rjk", cos_p, turned_im, precision=PRECISION_LEVEL) + jnp.einsum(
        "jp,rkp->rjk", sin_p, turned_re, precision=PRECISION_LEVEL
    )
    factor = 1.0 / math.sqrt(length)
    return (
        last_re.reshape(row_count, length) * factor,
        last_im.reshape(row_count, length) * factor,
    )


def transpose_global(real_part, imag_part):
    row_count, length = real_part.shape
    n_base = lax.axis_size("base")
    n_chan = lax.axis_size("chan")
    width = length // (n_base * n_chan)
    moved = (
        lax.all_to_all(
            lax.all_to_all(
                real_part.reshape(1, row_count, n_base, n_chan, width),
                "base",
                split_axis=2,
                concat_axis=0,
                tiled=True,
            ),
            "chan",
            split_axis=3,
            concat_axis=1,
            tiled=True,
        ),
        lax.all_to_all(
            lax.all_to_all(
                imag_part.reshape(1, row_count, n_base, n_chan, width),
                "base",
                split_axis=2,
                concat_axis=0,
                tiled=True,
            ),
            "chan",
            split_axis=3,
            concat_axis=1,
            tiled=True,
        ),
    )
    return (moved[0].reshape(length, width).T, moved[1].reshape(length, width).T)


def to_tiles(plane):
    row_count, length = plane.shape
    shaped = plane.reshape(row_count // TILE_V, TILE_V, length // TILE_U, TILE_U)
    return shaped.transpose(0, 2, 1, 3).reshape(-1, TILE_V * TILE_U)


def from_tiles(tiles, row_count, length):
    shaped = tiles.reshape(row_count // TILE_V, length // TILE_U, TILE_V, TILE_U)
    return shaped.transpose(0, 2, 1, 3).reshape(row_count, length)


def slot_work(sample_weights, masked_weight, sample_values):
    visible_samples = (
        jnp.einsum("gnz,gez->gen", sample_weights, sample_values, precision=PRECISION_LEVEL)
        * masked_weight[:, None, :]
    )
    return jnp.einsum("hbi,hyb->hyi", sample_weights, visible_samples, precision=PRECISION_LEVEL)


def total_squares(image):
    return lax.psum(jnp.sum(image * image), ("base", "chan"))


def per_device(image0, interp, vis_weight, counts, tile_index):
    n_base = lax.axis_size("base")
    n_chan = lax.axis_size("chan")
    row_count, length = image0.shape
    touch = tile_index.shape[2]
    slots_each = touch // (n_base * n_chan)
    vcap = interp.shape[3]
    cells = interp.shape[4]
    tiles_own = row_count // TILE_V * (length // TILE_U)
    live = (jnp.arange(vcap, dtype=jnp.int32)[None, :] < counts.reshape(touch, 1)).astype(
        jnp.float32
    )
    masked_weight = vis_weight.reshape(touch, vcap) * live
    sample_weights = interp.reshape(touch, vcap, cells)
    wanted = lax.all_to_all(
        lax.all_to_all(
            tile_index.reshape(n_base, n_chan, slots_each),
            "base",
            split_axis=0,
            concat_axis=0,
            tiled=True,
        ),
        "chan",
        split_axis=1,
        concat_axis=1,
        tiled=True,
    ).reshape(touch)
    onehot = (jnp.arange(tiles_own, dtype=jnp.int32)[:, None] == wanted[None, :]).astype(
        jnp.float32
    )
    moved = (
        lax.all_to_all(
            lax.all_to_all(
                sample_weights.reshape(n_base, n_chan, slots_each, vcap, cells),
                "base",
                split_axis=0,
                concat_axis=0,
                tiled=True,
            ),
            "chan",
            split_axis=1,
            concat_axis=1,
            tiled=True,
        ),
        lax.all_to_all(
            lax.all_to_all(
                masked_weight.reshape(n_base, n_chan, slots_each, vcap),
                "base",
                split_axis=0,
                concat_axis=0,
                tiled=True,
            ),
            "chan",
            split_axis=1,
            concat_axis=1,
            tiled=True,
        ),
    )
    sample_weights = moved[0].reshape(touch, vcap, cells)
    masked_weight = moved[1].reshape(touch, vcap)
    found = []
    current = image0 / jnp.sqrt(total_squares(image0))
    for iteration in range(ITERS):
        real_part, imag_part = transform_rows(current, None, -1.0)
        real_part, imag_part = transpose_global(real_part, imag_part)
        real_part, imag_part = transform_rows(real_part, imag_part, -1.0)
        tiles = jnp.stack([to_tiles(real_part), to_tiles(imag_part)], axis=1)
        sample_values = jnp.take(tiles, wanted, axis=0)
        gridded_plane = slot_work(sample_weights, masked_weight, sample_values)
        summed = jnp.einsum("ts,skc->tkc", onehot, gridded_plane, precision=PRECISION_LEVEL)
        real_part = from_tiles(summed[:, 0, :], row_count, length)
        imag_part = from_tiles(summed[:, 1, :], row_count, length)
        real_part, imag_part = transform_rows(real_part, imag_part, 1.0)
        real_part, imag_part = transpose_global(real_part, imag_part)
        real_part, imag_part = transform_rows(real_part, imag_part, 1.0)
        norm_value = jnp.sqrt(total_squares(real_part))
        found.append(norm_value)
        current = real_part / norm_value
    return (float(length) * current, jnp.stack(found))


def solution(mesh):
    placed = (
        P(("base", "chan"), None),
        P("base", "chan", None, None, None),
        P("base", "chan", None, None),
        P("base", "chan", None),
        P("base", "chan", None),
    )
    return jax.shard_map(
        per_device,
        mesh=mesh,
        in_specs=placed,
        out_specs=(P(("base", "chan"), None), P()),
        check_vma=False,
    )
```

profile of v0, /device:TPU:0, one launch (start us, length us, event | category | flops | bytes accessed | tf_op | source)
XLA Modules:
  0.0 998.7 jit_solution(13095551597312861529)
XLA Ops:
  3.3 7.4 all-to-all-start
  14.0 40.9 %psum.28 = f32[]{:T(128)} all-reduce(f32[]{:T(128)} %multiply_reduce_fusion.3), channel_id=1, replica_groups=mesh['base'=16,'chan'=2] {'base','chan'}, use_global_device_ids=true, to_apply=%region_1.0 | all-reduce | flops 1 | bytes 8 | tf_op jit(solution)/shard_map/psum | solution.py:109
  69.5 4.9 all-to-all-start.8
  81.7 6.5 all-to-all-start.2
  95.1 7.3 all-to-all-done.2
  111.5 9.4 all-to-all-done.4
  133.8 7.1 all-to-all-done.3
  140.9 10.1 %all_to_all.426 = f32[2,1,65536]{2,1,0:T(1,128)S(1)} all-to-all(f32[2,1,65536]{2,1,0:T(1,128)S(1)} %reshape.488), channel_id=1, replica_groups=mesh['base'=16,'chan'=2] {'chan'}, dimensions={0} | all-to-all | bytes 1048576 | tf_op jit(solution)/shard_map/all_to_all | solution.py:72
  151.1 4.9 all-to-all-start.6
  174.9 21.9 %all-to-all-done.6 = f32[16,2,8,8,256]{4,3,2,1,0:T(8,128)} async-done(((f32[16,2,8,8,256]{4,3,2,1,0:T(8,128)}), f32[16,2,8,8,256]{4,3,2,1,0:T(8,128)}, u32[]{:S(2)}, u32[]{:S(2)}) %all-to-all-start.6) | async-done | bytes 2097184 | tf_op jit(solution)/shard_map/all_to_all | solution.py:144
  200.0 4.8 all-to-all-start.7
  222.8 8.3 all-to-all-done.7
  266.8 10.7 %all-to-all-start.10 = ((f32[16,1,8192]{2,1,0:T(1,128)}), f32[16,1,8192]{2,1,0:T(1,128)}, u32[]{:S(2)}, u32[]{:S(2)}) async-start(f32[16,1,8192]{2,1,0:T(1,128)} %reshape.496), calls=%async_computation.10 | async-start | bytes 1048576 | tf_op jit(solution)/shard_map/all_to_all | solution.py:60
  291.9 4.2 all-to-all-start.12
  303.8 6.7 all-to-all-done.12
  323.3 4.4 all-to-all-start.13
  365.1 40.5 %psum.29 = f32[]{:T(128)} all-reduce(f32[]{:T(128)} %get-tuple-element.33), channel_id=1, replica_groups=mesh['base'=16,'chan'=2] {'base','chan'}, use_global_device_ids=true, to_apply=%region_3.5 | all-reduce | flops 1 | bytes 8 | tf_op jit(solution)/shard_map/psum | solution.py:109
  427.3 4.9 all-to-all-start.14
  458.3 6.7 all-to-all-done.16
  478.1 4.4 all-to-all-start.17
  580.5 4.5 all-to-all-start.18
  611.2 6.7 all-to-all-done.20
  631.0 4.4 all-to-all-start.21
  672.8 40.5 %psum.30 = f32[]{:T(128)} all-reduce(f32[]{:T(128)} %get-tuple-element.35), channel_id=1, replica_groups=mesh['base'=16,'chan'=2] {'base','chan'}, use_global_device_ids=true, to_apply=%region_5.7 | all-reduce | flops 1 | bytes 8 | tf_op jit(solution)/shard_map/psum | solution.py:109
  735.0 4.9 all-to-all-start.22
  766.0 6.7 all-to-all-done.24
  785.8 4.4 all-to-all-start.25
  876.3 4.4 all-to-all-start.26
  887.6 7.3 all-to-all-done.26
  903.8 9.5 all-to-all-done.28
  925.6 4.4 all-to-all-start.29
  955.4 40.5 %psum.31 = f32[]{:T(128)} all-reduce(f32[]{:T(128)} %get-tuple-element.37), channel_id=1, replica_groups=mesh['base'=16,'chan'=2] {'base','chan'}, use_global_device_ids=true, to_apply=%region_7.9 | all-reduce | flops 1 | bytes 8 | tf_op jit(solution)/shard_map/psum | solution.py:109
  (416 shorter events, 639.1 us)
Async XLA Ops:
  3.3 58.0 %all-to-all-start = ((s32[16,2,8]{2,1,0:T(2,128)}), s32[16,2,8]{2,1,0:T(2,128)S(1)}, u32[]{:S(2)}, u32[]{:S(2)}) async-start(s32[16,2,8]{2,1,0:T(2,128)} %reshape.396), calls=%async_computation | async-start | bytes 32768 | tf_op jit(solution)/shard_map/all_to_all | solution.py:127
  62.1 7.4 all-to-all-start.1
  69.5 12.2 %all-to-all-start.8 = ((f32[16,1,128]{2,1,0:T(1,128)}), f32[16,1,128]{2,1,0:T(1,128)S(1)}, u32[]{:S(2)}, u32[]{:S(2)}) async-start(f32[16,1,128]{2,1,0:T(1,128)} %reshape.492), calls=%async_computation.8 | async-start | bytes 16384 | tf_op jit(solution)/shard_map/all_to_all | solution.py:157
  81.7 20.7 %all-to-all-start.2 = ((f32[16,1,8192]{2,1,0:T(1,128)}), f32[16,1,8192]{2,1,0:T(1,128)S(1)}, u32[]{:S(2)}, u32[]{:S(2)}) async-start(f32[16,1,8192]{2,1,0:T(1,128)} %reshape.482), calls=%async_computation.2 | async-start | bytes 1048576 | tf_op jit(solution)/shard_map/all_to_all | solution.py:60
  102.4 18.4 %all-to-all-start.4 = ((f32[16,1,8192]{2,1,0:T(1,128)}), f32[16,1,8192]{2,1,0:T(1,128)S(1)}, u32[]{:S(2)}, u32[]{:S(2)}) async-start(f32[16,1,8192]{2,1,0:T(1,128)} %reshape.486), calls=%async_computation.4 | async-start | bytes 1048576 | tf_op jit(solution)/shard_map/all_to_all | solution.py:73
  120.9 8.0 all-to-all-start.9
  128.9 12.1 %all-to-all-start.3 = ((f32[2,1,65536]{2,1,0:T(1,128)}), f32[2,1,65536]{2,1,0:T(1,128)S(1)}, u32[]{:S(2)}, u32[]{:S(2)}) async-start(f32[2,1,65536]{2,1,0:T(1,128)} %reshape.484), calls=%async_computation.3 | async-start | bytes 1048576 | tf_op jit(solution)/shard_map/all_to_all | solution.py:59
  151.1 45.8 %all-to-all-start.6 = ((f32[16,2,8,8,256]{4,3,2,1,0:T(8,128)}), f32[16,2,8,8,256]{4,3,2,1,0:T(8,128)}, u32[]{:S(2)}, u32[]{:S(2)}) async-start(f32[16,2,8,8,256]{4,3,2,1,0:T(8,128)} %bitcast.810), calls=%async_computation.6 | async-start | bytes 4194304 | tf_op jit(solution)/shard_map/all_to_all | solution.py:144
  200.0 31.1 %all-to-all-start.7 = ((f32[16,2,8,8,256]{4,3,2,0,1:T(8,128)}), f32[16,2,8,8,256]{4,3,2,0,1:T(8,128)}, u32[]{:S(2)}, u32[]{:S(2)}) async-start(f32[16,2,8,8,256]{4,3,2,0,1:T(8,128)} %copy.493), calls=%async_computation.7 | async-start | bytes 4194304 | tf_op jit(solution)/shard_map/all_to_all | solution.py:143
  266.8 25.0 %all-to-all-start.10 = ((f32[16,1,8192]{2,1,0:T(1,128)}), f32[16,1,8192]{2,1,0:T(1,128)}, u32[]{:S(2)}, u32[]{:S(2)}) async-start(f32[16,1,8192]{2,1,0:T(1,128)} %reshape.496), calls=%async_computation.10 | async-start | bytes 1048576 | tf_op jit(solution)/shard_map/all_to_all | solution.py:60
  291.9 18.5 %all-to-all-start.12 = ((f32[16,1,8192]{2,1,0:T(1,128)}), f32[16,1,8192]{2,1,0:T(1,128)}, u32[]{:S(2)}, u32[]{:S(2)}) async-start(f32[16,1,8192]{2,1,0:T(1,128)} %reshape.500), calls=%async_computation.12 | async-start | bytes 1048576 | tf_op jit(solution)/shard_map/all_to_all | solution.py:73
  310.4 12.9 %all-to-all-start.11 = ((f32[2,1,65536]{2,1,0:T(1,128)}), f32[2,1,65536]{2,1,0:T(1,128)}, u32[]{:S(2)}, u32[]{:S(2)}) async-start(f32[2,1,65536]{2,1,0:T(1,128)} %reshape.498), calls=%async_computation.11 | async-start | bytes 1048576 | tf_op jit(solution)/shard_map/all_to_all | solution.py:59
  323.3 21.1 %all-to-all-start.13 = ((f32[2,1,65536]{2,1,0:T(1,128)}), f32[2,1,65536]{2,1,0:T(1,128)}, u32[]{:S(2)}, u32[]{:S(2)}) async-start(f32[2,1,65536]{2,1,0:T(1,128)} %reshape.502), calls=%async_computation.13 | async-start | bytes 1048576 | tf_op jit(solution)/shard_map/all_to_all | solution.py:72
  416.4 4.5 copy-start.4
  427.3 19.2 %all-to-all-start.14 = ((f32[16,1,8192]{2,1,0:T(1,128)}), f32[16,1,8192]{2,1,0:T(1,128)}, u32[]{:S(2)}, u32[]{:S(2)}) async-start(f32[16,1,8192]{2,1,0:T(1,128)} %reshape.504), calls=%async_computation.14 | async-start | bytes 1048576 | tf_op jit(solution)/shard_map/all_to_all | solution.py:60
  446.5 18.5 %all-to-all-start.16 = ((f32[16,1,8192]{2,1,0:T(1,128)}), f32[16,1,8192]{2,1,0:T(1,128)}, u32[]{:S(2)}, u32[]{:S(2)}) async-start(f32[16,1,8192]{2,1,0:T(1,128)} %reshape.508), calls=%async_computation.16 | async-start | bytes 1048576 | tf_op jit(solution)/shard_map/all_to_all | solution.py:73
  465.0 13.0 %all-to-all-start.15 = ((f32[2,1,65536]{2,1,0:T(1,128)}), f32[2,1,65536]{2,1,0:T(1,128)}, u32[]{:S(2)}, u32[]{:S(2)}) async-start(f32[2,1,65536]{2,1,0:T(1,128)} %reshape.506), calls=%async_computation.15 | async-start | bytes 1048576 | tf_op jit(solution)/shard_map/all_to_all | solution.py:59
  478.1 21.2 %all-to-all-start.17 = ((f32[2,1,65536]{2,1,0:T(1,128)}), f32[2,1,65536]{2,1,0:T(1,128)}, u32[]{:S(2)}, u32[]{:S(2)}) async-start(f32[2,1,65536]{2,1,0:T(1,128)} %reshape.510), calls=%async_computation.17 | async-start | bytes 1048576 | tf_op jit(solution)/shard_map/all_to_all | solution.py:72
  569.7 4.5 copy-start.1
  580.5 18.8 %all-to-all-start.18 = ((f32[16,1,8192]{2,1,0:T(1,128)}), f32[16,1,8192]{2,1,0:T(1,128)}, u32[]{:S(2)}, u32[]{:S(2)}) async-start(f32[16,1,8192]{2,1,0:T(1,128)} %reshape.512), calls=%async_computation.18 | async-start | bytes 1048576 | tf_op jit(solution)/shard_map/all_to_all | solution.py:60
  599.3 18.5 %all-to-all-start.20 = ((f32[16,1,8192]{2,1,0:T(1,128)}), f32[16,1,8192]{2,1,0:T(1,128)}, u32[]{:S(2)}, u32[]{:S(2)}) async-start(f32[16,1,8192]{2,1,0:T(1,128)} %reshape.516), calls=%async_computation.20 | async-start | bytes 1048576 | tf_op jit(solution)/shard_map/all_to_all | solution.py:73
  617.9 13.1 %all-to-all-start.19 = ((f32[2,1,65536]{2,1,0:T(1,128)}), f32[2,1,65536]{2,1,0:T(1,128)}, u32[]{:S(2)}, u32[]{:S(2)}) async-start(f32[2,1,65536]{2,1,0:T(1,128)} %reshape.514), calls=%async_computation.19 | async-start | bytes 1048576 | tf_op jit(solution)/shard_map/all_to_all | solution.py:59
  631.0 21.1 %all-to-all-start.21 = ((f32[2,1,65536]{2,1,0:T(1,128)}), f32[2,1,65536]{2,1,0:T(1,128)}, u32[]{:S(2)}, u32[]{:S(2)}) async-start(f32[2,1,65536]{2,1,0:T(1,128)} %reshape.518), calls=%async_computation.21 | async-start | bytes 1048576 | tf_op jit(solution)/shard_map/all_to_all | solution.py:72
  724.1 4.5 copy-start.5
  735.0 19.2 %all-to-all-start.22 = ((f32[16,1,8192]{2,1,0:T(1,128)}), f32[16,1,8192]{2,1,0:T(1,128)}, u32[]{:S(2)}, u32[]{:S(2)}) async-start(f32[16,1,8192]{2,1,0:T(1,128)} %reshape.520), calls=%async_computation.22 | async-start | bytes 1048576 | tf_op jit(solution)/shard_map/all_to_all | solution.py:60
  754.2 18.5 %all-to-all-start.24 = ((f32[16,1,8192]{2,1,0:T(1,128)}), f32[16,1,8192]{2,1,0:T(1,128)}, u32[]{:S(2)}, u32[]{:S(2)}) async-start(f32[16,1,8192]{2,1,0:T(1,128)} %reshape.524), calls=%async_computation.24 | async-start | bytes 1048576 | tf_op jit(solution)/shard_map/all_to_all | solution.py:73
  772.7 13.0 %all-to-all-start.23 = ((f32[2,1,65536]{2,1,0:T(1,128)}), f32[2,1,65536]{2,1,0:T(1,128)}, u32[]{:S(2)}, u32[]{:S(2)}) async-start(f32[2,1,65536]{2,1,0:T(1,128)} %reshape.522), calls=%async_computation.23 | async-start | bytes 1048576 | tf_op jit(solution)/shard_map/all_to_all | solution.py:59
  785.8 21.2 %all-to-all-start.25 = ((f32[2,1,65536]{2,1,0:T(1,128)}), f32[2,1,65536]{2,1,0:T(1,128)}, u32[]{:S(2)}, u32[]{:S(2)}) async-start(f32[2,1,65536]{2,1,0:T(1,128)} %reshape.526), calls=%async_computation.25 | async-start | bytes 1048576 | tf_op jit(solution)/shard_map/all_to_all | solution.py:72
  876.3 18.6 %all-to-all-start.26 = ((f32[16,1,8192]{2,1,0:T(1,128)}), f32[16,1,8192]{2,1,0:T(1,128)S(1)}, u32[]{:S(2)}, u32[]{:S(2)}) async-start(f32[16,1,8192]{2,1,0:T(1,128)} %reshape.528), calls=%async_computation.26 | async-start | bytes 1048576 | tf_op jit(solution)/shard_map/all_to_all | solution.py:60
  894.9 18.4 %all-to-all-start.28 = ((f32[16,1,8192]{2,1,0:T(1,128)}), f32[16,1,8192]{2,1,0:T(1,128)S(1)}, u32[]{:S(2)}, u32[]{:S(2)}) async-start(f32[16,1,8192]{2,1,0:T(1,128)} %reshape.532), calls=%async_computation.28 | async-start | bytes 1048576 | tf_op jit(solution)/shard_map/all_to_all | solution.py:73
  913.3 12.3 %all-to-all-start.27 = ((f32[2,1,65536]{2,1,0:T(1,128)}), f32[2,1,65536]{2,1,0:T(1,128)S(1)}, u32[]{:S(2)}, u32[]{:S(2)}) async-start(f32[2,1,65536]{2,1,0:T(1,128)} %reshape.530), calls=%async_computation.27 | async-start | bytes 1048576 | tf_op jit(solution)/shard_map/all_to_all | solution.py:59
  925.6 13.4 %all-to-all-start.29 = ((f32[2,1,65536]{2,1,0:T(1,128)}), f32[2,1,65536]{2,1,0:T(1,128)}, u32[]{:S(2)}, u32[]{:S(2)}) async-start(f32[2,1,65536]{2,1,0:T(1,128)} %reshape.534), calls=%async_computation.29 | async-start | bytes 1048576 | tf_op jit(solution)/shard_map/all_to_all | solution.py:72
  (15 other events, 38.1 us)
where the time goes:
time: 1010 us; the launch traced here: 999 us
  local copies, waits for them, and re-layouts  273 us (27%)
  matrix products  192 us (19%)
  blocking collectives  172 us (17%)
  starting transfers between devices  136 us (13%)
  waiting for transfers between devices  126 us (12%)
  other arithmetic  94.2 us (9%)
    psum x4, blocking collectives, total_squares(): return lax.psum(jnp.sum(image * image), ('base', 'chan'))  162 us
    unnamed x92, local copies, waits for them, and re-layouts  85.7 us
    all_to_all x6, waiting for transfers between devices, transpose_global(): lax.all_to_all(imag_part.reshape(1, row_count, n_base, n_chan, width), 'b...  45.5 us
    all_to_all x6, starting transfers between devices, transpose_global(): lax.all_to_all(real_part.reshape(1, row_count, n_base, n_chan, width), 'b...  35.7 us
    all_to_all x6, waiting for transfers between devices, transpose_global(): lax.all_to_all(real_part.reshape(1, row_count, n_base, n_chan, width), 'b...  31.4 us
    dot_general x12, matrix products, transform_rows(): jnp.einsum('jp,rkp->rjk', sin_p, turned_im, precision=PRECISION_LEVEL)  27.9 us
    all_to_all x6, starting transfers between devices, transpose_global(): lax.all_to_all(imag_part.reshape(1, row_count, n_base, n_chan, width), 'b...  25.3 us
    dot_general x12, matrix products, transform_rows(): jnp.einsum('kq,rqp->rkp', sin_q, real_in, precision=PRECISION_LEVEL)  24.4 us
  transfers between devices with their start and end apart: 29, of which 21 were waited for; matrix products, arithmetic and copies ran while one was open for 27% of the time, Pallas kernels for 0%

commit v1 on v0

--- a/solution.py
+++ b/solution.py
@@ -8,6 +8,13 @@
 TILE_U = 32
 ITERS = 3
 PRECISION_LEVEL = lax.Precision.HIGHEST
+
+
+def trade_parts(x, axis, split, join):
+    devices = lax.axis_size(axis)
+    blocks = jnp.stack(jnp.split(x, devices, axis=split), axis=0)
+    blocks = lax.all_to_all(blocks, axis, split_axis=0, concat_axis=0)
+    return jnp.concatenate(blocks, axis=join)
 
 
 def split_length(length):
@@ -70,13 +77,7 @@
             tiled=True,
         ),
         lax.all_to_all(
-            lax.all_to_all(
-                imag_part.reshape(1, row_count, n_base, n_chan, width),
-                "base",
-                split_axis=2,
-                concat_axis=0,
-                tiled=True,
-            ),
+            trade_parts(imag_part.reshape(1, row_count, n_base, n_chan, width), "base", 2, 0),
             "chan",
             split_axis=3,
             concat_axis=1,

time: 1010 us -> 1100 us (1.089)
  local copies, waits for them, and re-layouts: 273 us -> 376 us
  matrix products: 192 us -> 176 us
    unnamed x92 -> x306, local copies, waits for them, and re-layouts: 85.7 us -> 195 us
    mul x9 -> x3, local copies, waits for them, and re-layouts: 20.7 us -> 7.06 us  [transform_rows(): last_im.reshape(row_count, length) * factor]
  transfers between devices with their start and end apart: 29 -> 29, of which waited for: 21 -> 18; matrix products, arithmetic and copies ran while one was open for 27% -> 31% of each run, Pallas kernels for 0% -> 0%
where the time goes in v1:
time: 1100 us; the launch traced here: 1090 us
  local copies, waits for them, and re-layouts  376 us (34%)
  matrix products  176 us (16%)
  blocking collectives  172 us (16%)
  starting transfers between devices  142 us (13%)
  waiting for transfers between devices  123 us (11%)
  other arithmetic  90 us (8%)
    unnamed x306, local copies, waits for them, and re-layouts  195 us
    psum x4, blocking collectives, total_squares(): return lax.psum(jnp.sum(image * image), ('base', 'chan'))  162 us
    all_to_all x6, waiting for transfers between devices, trade_parts(): blocks = lax.all_to_all(blocks, axis, split_axis=0, concat_axis=0)  49.5 us
    all_to_all x6, starting transfers between devices, transpose_global(): lax.all_to_all(real_part.reshape(1, row_count, n_base, n_chan, width), 'b...  34.1 us
    all_to_all x6, starting transfers between devices, trade_parts(): blocks = lax.all_to_all(blocks, axis, split_axis=0, concat_axis=0)  32.7 us
    dot_general x12, matrix products, transform_rows(): jnp.einsum('jp,rkp->rjk', sin_p, turned_im, precision=PRECISION_LEVEL)  26.7 us
    all_to_all x6, starting transfers between devices, transpose_global(): lax.all_to_all(lax.all_to_all(real_part.reshape(1, row_count, n_base, n_c...  23.8 us
    dot_general x9, matrix products, transform_rows(): jnp.einsum('kq,rqp->rkp', sin_q, imag_in, precision=PRECISION_LEVEL)  23.1 us
  transfers between devices with their start and end apart: 29, of which 18 were waited for; matrix products, arithmetic and copies ran while one was open for 31% of the time, Pallas kernels for 0%

profile of v1, /device:TPU:0, one launch (start us, length us, event | category | flops | bytes accessed | tf_op | source)
XLA Modules:
  0.0 1085.4 jit_solution(7341168562022338400)
XLA Ops:
  3.1 7.4 all-to-all-start
  13.8 40.9 %psum.28 = f32[]{:T(128)} all-reduce(f32[]{:T(128)} %multiply_reduce_fusion.3), channel_id=1, replica_groups=mesh['base'=16,'chan'=2] {'base','chan'}, use_global_device_ids=true, to_apply=%region_1.0 | all-reduce | flops 1 | bytes 8 | tf_op jit(solution)/shard_map/psum | solution.py:110
  76.8 4.9 all-to-all-start.8
  94.1 11.8 %all-to-all-done.2 = f32[16,1,8192]{2,1,0:T(1,128)S(1)} async-done(((f32[16,1,8192]{2,1,0:T(1,128)}), f32[16,1,8192]{2,1,0:T(1,128)S(1)}, u32[]{:S(2)}, u32[]{:S(2)}) %all-to-all-start.2) | async-done | bytes 524320 | tf_op jit(solution)/shard_map/all_to_all | solution.py:67
  115.0 9.4 all-to-all-done.4
  137.2 7.1 all-to-all-done.3
  144.4 10.1 all_to_all.348
  154.5 4.9 all-to-all-start.6
  178.4 21.9 %all-to-all-done.6 = f32[16,2,8,8,256]{4,3,2,1,0:T(8,128)} async-done(((f32[16,2,8,8,256]{4,3,2,1,0:T(8,128)}), f32[16,2,8,8,256]{4,3,2,1,0:T(8,128)}, u32[]{:S(2)}, u32[]{:S(2)}) %all-to-all-start.6) | async-done | bytes 2097184 | tf_op jit(solution)/shard_map/all_to_all | solution.py:145
  203.4 4.8 all-to-all-start.7
  226.2 8.3 all-to-all-done.7
  273.0 11.2 %all-to-all-start.10 = ((f32[16,1,8192]{2,1,0:T(1,128)}), f32[16,1,8192]{2,1,0:T(1,128)S(1)}, u32[]{:S(2)}, u32[]{:S(2)}) async-start(f32[16,1,8192]{2,1,0:T(1,128)} %reshape.520), calls=%async_computation.10 | async-start | bytes 1048576 | tf_op jit(solution)/shard_map/all_to_all | solution.py:67
  314.4 6.2 all-to-all-start.12
  327.2 7.6 all-to-all-done.12
  389.5 40.5 %psum.29 = f32[]{:T(128)} all-reduce(f32[]{:T(128)} %get-tuple-element.129), channel_id=1, replica_groups=mesh['base'=16,'chan'=2] {'base','chan'}, use_global_device_ids=true, to_apply=%region_3.5 | all-reduce | flops 1 | bytes 8 | tf_op jit(solution)/shard_map/psum | solution.py:110
  454.1 4.8 all-to-all-start.14
  489.1 6.1 all-to-all-start.16
  501.8 7.6 all-to-all-done.16
  522.3 4.4 all-to-all-start.17
  626.9 5.0 all-to-all-start.18
  662.0 6.2 all-to-all-start.20
  674.9 7.6 all-to-all-done.20
  695.6 4.4 all-to-all-start.21
  737.4 40.5 %psum.30 = f32[]{:T(128)} all-reduce(f32[]{:T(128)} %get-tuple-element.131), channel_id=1, replica_groups=mesh['base'=16,'chan'=2] {'base','chan'}, use_global_device_ids=true, to_apply=%region_5.7 | all-reduce | flops 1 | bytes 8 | tf_op jit(solution)/shard_map/psum | solution.py:110
  802.1 4.8 all-to-all-start.22
  837.0 6.1 all-to-all-start.24
  849.7 7.6 all-to-all-done.24
  870.3 4.4 all-to-all-start.25
  962.6 4.8 all-to-all-start.26
  971.2 10.4 all-to-all-done.26
  990.6 9.5 all-to-all-done.28
  1042.1 40.5 %psum.31 = f32[]{:T(128)} all-reduce(f32[]{:T(128)} %get-tuple-element.133), channel_id=1, replica_groups=mesh['base'=16,'chan'=2] {'base','chan'}, use_global_device_ids=true, to_apply=%region_7.9 | all-reduce | flops 1 | bytes 8 | tf_op jit(solution)/shard_map/psum | solution.py:110
  (636 shorter events, 707.4 us)
Async XLA Ops:
  0.6 54.7 %copy-start.31 = (s32[1,1,256]{2,1,0:T(1,128)S(1)}, s32[1,1,256]{2,1,0:T(1,128)}, u32[]{:S(2)}) copy-start(s32[1,1,256]{2,1,0:T(1,128)} %param.10) | copy-start | bytes 3076
  0.6 55.4 %copy-start.30 = (f32[1,1,256,8]{2,3,1,0:T(8,128)S(1)}, f32[1,1,256,8]{2,3,1,0:T(8,128)}, u32[]{:S(2)}) copy-start(f32[1,1,256,8]{2,3,1,0:T(8,128)} %param.9) | copy-start | bytes 24580
  3.1 65.5 %all-to-all-start = ((s32[16,2,8]{2,1,0:T(2,128)}), s32[16,2,8]{2,1,0:T(2,128)S(1)}, u32[]{:S(2)}, u32[]{:S(2)}) async-start(s32[16,2,8]{2,1,0:T(2,128)} %reshape.414), calls=%async_computation | async-start | bytes 32768 | tf_op jit(solution)/shard_map/all_to_all | solution.py:128
  69.3 7.4 all-to-all-start.1
  76.8 11.4 %all-to-all-start.8 = ((f32[16,1,128]{2,1,0:T(1,128)}), f32[16,1,128]{2,1,0:T(1,128)S(1)}, u32[]{:S(2)}, u32[]{:S(2)}) async-start(f32[16,1,128]{2,1,0:T(1,128)} %reshape.516), calls=%async_computation.8 | async-start | bytes 16384 | tf_op jit(solution)/shard_map/all_to_all | solution.py:158
  88.1 17.8 %all-to-all-start.2 = ((f32[16,1,8192]{2,1,0:T(1,128)}), f32[16,1,8192]{2,1,0:T(1,128)S(1)}, u32[]{:S(2)}, u32[]{:S(2)}) async-start(f32[16,1,8192]{2,1,0:T(1,128)} %reshape.506), calls=%async_computation.2 | async-start | bytes 1048576 | tf_op jit(solution)/shard_map/all_to_all | solution.py:67
  106.0 18.4 %all-to-all-start.4 = ((f32[16,1,8192]{2,1,0:T(1,128)}), f32[16,1,8192]{2,1,0:T(1,128)S(1)}, u32[]{:S(2)}, u32[]{:S(2)}) async-start(f32[16,1,8192]{2,1,0:T(1,128)} %reshape.510), calls=%async_computation.4 | async-start | bytes 1048576 | tf_op jit(solution)/shard_map/all_to_all | solution.py:16
  124.3 8.0 all-to-all-start.9
  132.3 12.1 %all-to-all-start.3 = ((f32[2,1,65536]{2,1,0:T(1,128)}), f32[2,1,65536]{2,1,0:T(1,128)S(1)}, u32[]{:S(2)}, u32[]{:S(2)}) async-start(f32[2,1,65536]{2,1,0:T(1,128)} %reshape.508), calls=%async_computation.3 | async-start | bytes 1048576 | tf_op jit(solution)/shard_map/all_to_all | solution.py:66
  154.5 45.8 %all-to-all-start.6 = ((f32[16,2,8,8,256]{4,3,2,1,0:T(8,128)}), f32[16,2,8,8,256]{4,3,2,1,0:T(8,128)}, u32[]{:S(2)}, u32[]{:S(2)}) async-start(f32[16,2,8,8,256]{4,3,2,1,0:T(8,128)} %bitcast.972), calls=%async_computation.6 | async-start | bytes 4194304 | tf_op jit(solution)/shard_map/all_to_all | solution.py:145
  203.4 31.2 %all-to-all-start.7 = ((f32[16,2,8,8,256]{4,3,2,0,1:T(8,128)}), f32[16,2,8,8,256]{4,3,2,0,1:T(8,128)}, u32[]{:S(2)}, u32[]{:S(2)}) async-start(f32[16,2,8,8,256]{4,3,2,0,1:T(8,128)} %copy.868), calls=%async_computation.7 | async-start | bytes 4194304 | tf_op jit(solution)/shard_map/all_to_all | solution.py:144
  273.0 35.3 %copy-start.10 = (f32[1,64,1,2,64]{4,3,2,1,0:T(2,128)S(1)}, f32[1,64,1,2,64]{4,3,2,1,0:T(2,128)}, u32[]{:S(2)}) copy-start(f32[1,64,1,2,64]{4,3,2,1,0:T(2,128)} %get-tuple-element.95) | copy-start | bytes 98308
  273.0 41.3 %all-to-all-start.10 = ((f32[16,1,8192]{2,1,0:T(1,128)}), f32[16,1,8192]{2,1,0:T(1,128)S(1)}, u32[]{:S(2)}, u32[]{:S(2)}) async-start(f32[16,1,8192]{2,1,0:T(1,128)} %reshape.520), calls=%async_computation.10 | async-start | bytes 1048576 | tf_op jit(solution)/shard_map/all_to_all | solution.py:67
  314.4 20.5 %all-to-all-start.12 = ((f32[16,1,8192]{2,1,0:T(1,128)}), f32[16,1,8192]{2,1,0:T(1,128)}, u32[]{:S(2)}, u32[]{:S(2)}) async-start(f32[16,1,8192]{2,1,0:T(1,128)} %reshape.524), calls=%async_computation.12 | async-start | bytes 1048576 | tf_op jit(solution)/shard_map/all_to_all | solution.py:16
  334.9 12.9 %all-to-all-start.11 = ((f32[2,1,65536]{2,1,0:T(1,128)}), f32[2,1,65536]{2,1,0:T(1,128)}, u32[]{:S(2)}, u32[]{:S(2)}) async-start(f32[2,1,65536]{2,1,0:T(1,128)} %reshape.522), calls=%async_computation.11 | async-start | bytes 1048576 | tf_op jit(solution)/shard_map/all_to_all | solution.py:66
  347.7 21.1 %all-to-all-start.13 = ((f32[2,1,65536]{2,1,0:T(1,128)}), f32[2,1,65536]{2,1,0:T(1,128)}, u32[]{:S(2)}, u32[]{:S(2)}) async-start(f32[2,1,65536]{2,1,0:T(1,128)} %reshape.526), calls=%async_computation.13 | async-start | bytes 1048576 | tf_op jit(solution)/shard_map/all_to_all | solution.py:79
  454.1 34.9 %all-to-all-start.14 = ((f32[16,1,8192]{2,1,0:T(1,128)}), f32[16,1,8192]{2,1,0:T(1,128)S(1)}, u32[]{:S(2)}, u32[]{:S(2)}) async-start(f32[16,1,8192]{2,1,0:T(1,128)} %reshape.528), calls=%async_computation.14 | async-start | bytes 1048576 | tf_op jit(solution)/shard_map/all_to_all | solution.py:67
  489.1 20.4 %all-to-all-start.16 = ((f32[16,1,8192]{2,1,0:T(1,128)}), f32[16,1,8192]{2,1,0:T(1,128)}, u32[]{:S(2)}, u32[]{:S(2)}) async-start(f32[16,1,8192]{2,1,0:T(1,128)} %reshape.532), calls=%async_computation.16 | async-start | bytes 1048576 | tf_op jit(solution)/shard_map/all_to_all | solution.py:16
  509.5 12.9 %all-to-all-start.15 = ((f32[2,1,65536]{2,1,0:T(1,128)}), f32[2,1,65536]{2,1,0:T(1,128)}, u32[]{:S(2)}, u32[]{:S(2)}) async-start(f32[2,1,65536]{2,1,0:T(1,128)} %reshape.530), calls=%async_computation.15 | async-start | bytes 1048576 | tf_op jit(solution)/shard_map/all_to_all | solution.py:66
  522.3 21.1 %all-to-all-start.17 = ((f32[2,1,65536]{2,1,0:T(1,128)}), f32[2,1,65536]{2,1,0:T(1,128)}, u32[]{:S(2)}, u32[]{:S(2)}) async-start(f32[2,1,65536]{2,1,0:T(1,128)} %reshape.534), calls=%async_computation.17 | async-start | bytes 1048576 | tf_op jit(solution)/shard_map/all_to_all | solution.py:79
  626.9 35.1 %all-to-all-start.18 = ((f32[16,1,8192]{2,1,0:T(1,128)}), f32[16,1,8192]{2,1,0:T(1,128)S(1)}, u32[]{:S(2)}, u32[]{:S(2)}) async-start(f32[16,1,8192]{2,1,0:T(1,128)} %reshape.536), calls=%async_computation.18 | async-start | bytes 1048576 | tf_op jit(solution)/shard_map/all_to_all | solution.py:67
  662.0 20.5 %all-to-all-start.20 = ((f32[16,1,8192]{2,1,0:T(1,128)}), f32[16,1,8192]{2,1,0:T(1,128)}, u32[]{:S(2)}, u32[]{:S(2)}) async-start(f32[16,1,8192]{2,1,0:T(1,128)} %reshape.540), calls=%async_computation.20 | async-start | bytes 1048576 | tf_op jit(solution)/shard_map/all_to_all | solution.py:16
  682.5 13.1 %all-to-all-start.19 = ((f32[2,1,65536]{2,1,0:T(1,128)}), f32[2,1,65536]{2,1,0:T(1,128)}, u32[]{:S(2)}, u32[]{:S(2)}) async-start(f32[2,1,65536]{2,1,0:T(1,128)} %reshape.538), calls=%async_computation.19 | async-start | bytes 1048576 | tf_op jit(solution)/shard_map/all_to_all | solution.py:66
  695.6 21.1 %all-to-all-start.21 = ((f32[2,1,65536]{2,1,0:T(1,128)}), f32[2,1,65536]{2,1,0:T(1,128)}, u32[]{:S(2)}, u32[]{:S(2)}) async-start(f32[2,1,65536]{2,1,0:T(1,128)} %reshape.542), calls=%async_computation.21 | async-start | bytes 1048576 | tf_op jit(solution)/shard_map/all_to_all | solution.py:79
  802.1 34.9 %all-to-all-start.22 = ((f32[16,1,8192]{2,1,0:T(1,128)}), f32[16,1,8192]{2,1,0:T(1,128)S(1)}, u32[]{:S(2)}, u32[]{:S(2)}) async-start(f32[16,1,8192]{2,1,0:T(1,128)} %reshape.544), calls=%async_computation.22 | async-start | bytes 1048576 | tf_op jit(solution)/shard_map/all_to_all | solution.py:67
  837.0 20.4 %all-to-all-start.24 = ((f32[16,1,8192]{2,1,0:T(1,128)}), f32[16,1,8192]{2,1,0:T(1,128)}, u32[]{:S(2)}, u32[]{:S(2)}) async-start(f32[16,1,8192]{2,1,0:T(1,128)} %reshape.548), calls=%async_computation.24 | async-start | bytes 1048576 | tf_op jit(solution)/shard_map/all_to_all | solution.py:16
  857.4 12.9 %all-to-all-start.23 = ((f32[2,1,65536]{2,1,0:T(1,128)}), f32[2,1,65536]{2,1,0:T(1,128)}, u32[]{:S(2)}, u32[]{:S(2)}) async-start(f32[2,1,65536]{2,1,0:T(1,128)} %reshape.546), calls=%async_computation.23 | async-start | bytes 1048576 | tf_op jit(solution)/shard_map/all_to_all | solution.py:66
  870.3 21.1 %all-to-all-start.25 = ((f32[2,1,65536]{2,1,0:T(1,128)}), f32[2,1,65536]{2,1,0:T(1,128)}, u32[]{:S(2)}, u32[]{:S(2)}) async-start(f32[2,1,65536]{2,1,0:T(1,128)} %reshape.550), calls=%async_computation.25 | async-start | bytes 1048576 | tf_op jit(solution)/shard_map/all_to_all | solution.py:79
  962.6 19.1 %all-to-all-start.26 = ((f32[16,1,8192]{2,1,0:T(1,128)}), f32[16,1,8192]{2,1,0:T(1,128)S(1)}, u32[]{:S(2)}, u32[]{:S(2)}) async-start(f32[16,1,8192]{2,1,0:T(1,128)} %reshape.552), calls=%async_computation.26 | async-start | bytes 1048576 | tf_op jit(solution)/shard_map/all_to_all | solution.py:67
  981.7 18.4 %all-to-all-start.28 = ((f32[16,1,8192]{2,1,0:T(1,128)}), f32[16,1,8192]{2,1,0:T(1,128)S(1)}, u32[]{:S(2)}, u32[]{:S(2)}) async-start(f32[16,1,8192]{2,1,0:T(1,128)} %reshape.556), calls=%async_computation.28 | async-start | bytes 1048576 | tf_op jit(solution)/shard_map/all_to_all | solution.py:16
  1000.1 12.3 %all-to-all-start.27 = ((f32[2,1,65536]{2,1,0:T(1,128)}), f32[2,1,65536]{2,1,0:T(1,128)S(1)}, u32[]{:S(2)}, u32[]{:S(2)}) async-start(f32[2,1,65536]{2,1,0:T(1,128)} %reshape.554), calls=%async_computation.27 | async-start | bytes 1048576 | tf_op jit(solution)/shard_map/all_to_all | solution.py:66
  1012.4 13.3 %all-to-all-start.29 = ((f32[2,1,65536]{2,1,0:T(1,128)}), f32[2,1,65536]{2,1,0:T(1,128)}, u32[]{:S(2)}, u32[]{:S(2)}) async-start(f32[2,1,65536]{2,1,0:T(1,128)} %reshape.558), calls=%async_computation.29 | async-start | bytes 1048576 | tf_op jit(solution)/shard_map/all_to_all | solution.py:79
  (29 other events, 411.1 us)
